TPU v7x, 256 devices: a whole 4x4x8 slice. The times are simulated.
256 devices in a mesh: rep: 2 (over z_hi), dp: 32 (over z_lo, x, core), mp: 4 (over y).
Axes of the slice: x: 4, y: 4, z: 8 (z_hi: 2, z_lo: 4; z = z_hi * 4 + z_lo), core: 2. Of those that a mesh axis runs over, the one named last changes fastest.
Arguments:
- tokens: bfloat16 [24576, 2048], P(('rep', 'dp', 'mp')), may hold values from -6 to 6
- request_ids: int32 [64, 384], P(('rep', 'dp')), may hold values from 0 to 7, never falling along the last dimension, each value on 1 to 192 neighbouring positions
- cache_entries: bfloat16 [32768, 4096], P(('rep', 'dp', 'mp')), may hold values from -250 to 250, as said below
- cached_lengths: int32 [64, 8], replicated, may hold values from 1 to 256, 512 in all within a row
- traded: int32 [32], P('dp'), may hold values from 0 to 1, as said below
- query_weight: bfloat16 [2048, 2048], P(None, 'mp'), may hold values from -0.125 to 0.125
- key_weight: bfloat16 [2048, 2048], P(None, 'mp'), may hold values from -0.125 to 0.125
- value_weight: bfloat16 [2048, 2048], P(None, 'mp'), may hold values from -0.125 to 0.125
- output_weight: bfloat16 [2048, 2048], P('mp'), may hold values from -0.125 to 0.125
- gate_weight: bfloat16 [2048, 8192], P('dp', 'mp'), may hold values from -0.125 to 0.125
- up_weight: bfloat16 [2048, 8192], P('dp', 'mp'), may hold values from -0.125 to 0.125
- down_weight: bfloat16 [2048, 8192], P('dp', 'mp'), may hold values from -0.0625 to 0.0625
Outputs:
- layer_output: bfloat16 [24576, 2048], P(('rep', 'dp', 'mp'))
Inputs may be any that keep to these rules, and one draw needn't show every extreme that they name: `request_ids`: each group's row never falls; every request 0 to 7 has 1 to 192 new tokens in each group, some request exactly 192. `cached_lengths`: each row sums to 512; its largest entry is 256. `traded`: exactly 16 entries are 1. `cache_entries`: keys are stored already rotated to their positions; rows of cache group g are g * 512 to (g + 1) * 512 - 1, the requests' prefixes in request order.
All inputs are finite; a program needn't handle non-finite values.
Results may differ from a plain program's by a relative error of at most 0.013.
The roundings to bfloat16 on the way count: a program that leaves them out, or rounds other values in their place, can miss the bound.
Values may be sent and summed in bfloat16 or wider, within the bound.
A program may use at most 128 MiB of HBM per device.

v0:
```python
import math

import jax
import jax.numpy as jnp
from jax import lax
from jax.sharding import PartitionSpec as P

D = 2048
HEADS = 16
HEAD_DIM = 128
TOK_GROUP = 384
CACHE = 512


EPSILON = 1e-05
ROPE_BASE = 10000.0


def swapped(value, axis, apart):
    mask = 2**apart
    pairs = [(source, source ^ mask) for source in range(lax.axis_size(axis))]
    return lax.ppermute(value, axis, pairs)


def layer_norm(rows):
    center = rows - jnp.mean(rows, axis=-1, keepdims=True)
    spread = jnp.mean(center * center, axis=-1, keepdims=True)
    return center * lax.rsqrt(spread + EPSILON)


def request_layout(request_row, length_row, cache_size):
    number = length_row.shape[0]
    labels = jnp.arange(number, dtype=jnp.int32)
    onehot = (request_row[:, None] == labels[None, :]).astype(jnp.int32)
    counts = jnp.sum(onehot, axis=0)
    starts = jnp.cumsum(counts) - counts
    token_place = jnp.arange(request_row.shape[0], dtype=jnp.int32)
    positions = jnp.sum(onehot * (length_row - starts)[None, :], axis=1) + token_place
    bounds = jnp.cumsum(length_row)
    cache_place = jnp.arange(cache_size, dtype=jnp.int32)
    owner = jnp.sum((cache_place[:, None] >= bounds[None, :]).astype(jnp.int32), axis=1)
    return (positions, owner)


def rotate(vectors, positions):
    half = vectors.shape[-1] // 2
    freq = ROPE_BASE ** (-jnp.arange(half, dtype=jnp.float32) / half)
    angle = positions.astype(jnp.float32)[:, None] * freq[None, :]
    cosine = jnp.cos(angle)[:, None, :]
    sine = jnp.sin(angle)[:, None, :]
    first = vectors[..., :half]
    second = vectors[..., half:]
    return jnp.concatenate(
        [first * cosine - second * sine, second * cosine + first * sine], axis=-1
    )


def attend(query, keys_new, values_new, keys_cache, values_cache, request_row, owner):
    scale = 1.0 / math.sqrt(query.shape[-1])
    keys = jnp.concatenate([keys_cache, keys_new], axis=0)
    values = jnp.concatenate([values_cache, values_new], axis=0)
    scores = jnp.einsum("thd,khd->htk", query, keys, preferred_element_type=jnp.float32) * scale
    count = request_row.shape[0]
    place = jnp.arange(count, dtype=jnp.int32)
    same_cache = owner[None, :] == request_row[:, None]
    same_new = (request_row[None, :] == request_row[:, None]) & (place[None, :] <= place[:, None])
    allowed = jnp.concatenate([same_cache, same_new], axis=1)
    scores = jnp.where(allowed[None], scores, -1e30)
    top = jnp.max(scores, axis=-1, keepdims=True)
    raised = jnp.exp(scores - top)
    total = jnp.sum(raised, axis=-1, keepdims=True)
    weights = (raised / total).astype(jnp.bfloat16)
    mixed = jnp.einsum("htk,khd->thd", weights, values, preferred_element_type=jnp.float32)
    return mixed.astype(jnp.bfloat16)


def local(
    tokens,
    request_ids,
    cache_entries,
    cached_lengths,
    traded,
    query_weight,
    key_weight,
    value_weight,
    output_weight,
    gate_weight,
    up_weight,
    down_weight,
):
    tensor_size = lax.axis_size("mp")
    local_heads = HEADS // tensor_size
    replica = lax.axis_index("rep")
    within = lax.axis_index("dp")
    pairs = lax.axis_size("dp")
    group = replica * pairs + within
    moved_here = traded[0] == 1
    source = jnp.where(moved_here, (1 - replica) * pairs + within, group)
    length_row = lax.dynamic_slice_in_dim(cached_lengths, source, 1, 0)[0]
    request_row = request_ids[0]
    partner = swapped(cache_entries, "rep", 0)
    stored = jnp.where(moved_here, partner, cache_entries)
    by_heads = lax.all_to_all(
        stored.reshape(stored.shape[0], 2, D), "mp", split_axis=2, concat_axis=0, tiled=True
    )
    keys_cache = by_heads[:, 0].reshape(CACHE, local_heads, HEAD_DIM)
    values_cache = by_heads[:, 1].reshape(CACHE, local_heads, HEAD_DIM)
    rows_full = lax.all_gather(tokens, "mp", axis=0, tiled=True)
    positions, owner = request_layout(request_row, length_row, CACHE)
    normed = layer_norm(rows_full.astype(jnp.float32)).astype(jnp.bfloat16)
    query = jnp.dot(normed, query_weight, preferred_element_type=jnp.float32).reshape(
        TOK_GROUP, local_heads, HEAD_DIM
    )
    query = rotate(query, positions).astype(jnp.bfloat16)
    keys_new = jnp.dot(normed, key_weight, preferred_element_type=jnp.float32).reshape(
        TOK_GROUP, local_heads, HEAD_DIM
    )
    keys_new = rotate(keys_new, positions).astype(jnp.bfloat16)
    values_new = (
        jnp.dot(normed, value_weight, preferred_element_type=jnp.float32)
        .astype(jnp.bfloat16)
        .reshape(TOK_GROUP, local_heads, HEAD_DIM)
    )
    mixed = attend(query, keys_new, values_new, keys_cache, values_cache, request_row, owner)
    mixed = mixed.reshape(TOK_GROUP, local_heads * HEAD_DIM)
    own_sum = lax.psum_scatter(
        jnp.dot(mixed, output_weight, preferred_element_type=jnp.float32),
        "mp",
        scatter_dimension=0,
        tiled=True,
    )
    state_own = (tokens.astype(jnp.float32) + own_sum).astype(jnp.bfloat16)
    normed_own = layer_norm(state_own.astype(jnp.float32)).astype(jnp.bfloat16)
    normed_two = lax.all_gather(normed_own, "mp", axis=0, tiled=True)

    def add_rows(piece):
        return jnp.dot(normed_two, piece, preferred_element_type=jnp.float32)

    gate = add_rows(lax.all_gather(gate_weight, "dp", axis=0, tiled=True))
    upward = add_rows(lax.all_gather(up_weight, "dp", axis=0, tiled=True))
    activated = (jax.nn.silu(gate) * upward).astype(jnp.bfloat16)
    terms = lax.dot_general(
        activated,
        lax.all_gather(down_weight, "dp", axis=0, tiled=True),
        (((1,), (1,)), ((), ())),
        preferred_element_type=jnp.float32,
    )
    hidden_own = lax.psum_scatter(terms, "mp", scatter_dimension=0, tiled=True)
    return (state_own.astype(jnp.float32) + hidden_own).astype(jnp.bfloat16)


def solution(mesh):
    in_specs = (
        P(("rep", "dp", "mp"), None),
        P(("rep", "dp"), None),
        P(("rep", "dp", "mp"), None),
        P(),
        P("dp"),
        P(None, "mp"),
        P(None, "mp"),
        P(None, "mp"),
        P("mp", None),
        P("dp", "mp"),
        P("dp", "mp"),
        P("dp", "mp"),
    )
    out_specs = P(("rep", "dp", "mp"), None)
    return jax.shard_map(local, mesh=mesh, in_specs=in_specs, out_specs=out_specs, check_vma=False)
```

profile of v0, /device:TPU:1, one launch (start us, length us, event | category | flops | bytes accessed | tf_op | source)
XLA Modules:
  0.0 476.3 jit_solution(9177185737929228484)
XLA Ops:
  6.5 1.8 copy.71
  8.3 7.8 %collective-permute-start = (bf16[128,4096]{0,1:T(8,128)(2,1)S(1)}, bf16[128,4096]{0,1:T(8,128)(2,1)}, u32[]{:S(2)}, u32[]{:S(2)}) collective-permute-start(bf16[128,4096]{0,1:T(8,128)(2,1)S(1)} %copy.71), channel_id=1, source_target_pairs={{0,128},{128,0},{1,129},{129,1},{2,130},{130,2},{3,131},{131,3},{4... | collective-permute-start | bytes 3145736 | tf_op jit(solution)/shard_map/ppermute | solution.py:22
  16.1 0.0 all-gather.6.cloned.1.call-update
  16.8 0.8 constant_dynamic-slice_fusion
  17.6 0.1 copy.86
  17.7 0.7 reduce
  18.4 0.1 convert_reduce_fusion.3
  18.5 0.2 reduce-window_1_clone.1
  18.7 0.2 reduce-window.9
  18.8 0.1 convert_reduce_fusion.2
  18.9 0.1 select_reduce_fusion
  19.0 0.2 broadcast_compare_fusion
  19.2 25.3 %collective-permute-done = bf16[128,4096]{0,1:T(8,128)(2,1)} collective-permute-done((bf16[128,4096]{0,1:T(8,128)(2,1)S(1)}, bf16[128,4096]{0,1:T(8,128)(2,1)}, u32[]{:S(2)}, u32[]{:S(2)}) %collective-permute-start) | collective-permute-done | bytes 1048608 | tf_op jit(solution)/shard_map/ppermute | solution.py:22
  44.6 0.1 broadcast_select_fusion
  44.7 9.5 %copy.73 = bf16[128,2,2048]{0,1,2:T(2,128)(2,1)} copy(bf16[128,2,2048]{0,2,1:T(8,128)(2,1)S(1)} %bitcast.28) | data formatting | bytes 2097152 | tf_op jit(solution)/shard_map/reshape | solution.py:104
  54.1 4.7 all-to-all-start
  58.9 0.1 fusion.26
  59.0 0.8 pad_add_fusion
  59.8 1.5 multiply_cosine_fusion
  61.3 7.3 %all-to-all-done = bf16[128,2,2048]{0,1,2:T(2,128)(2,1)S(1)} async-done(((bf16[128,2,2048]{0,1,2:T(2,128)(2,1)}), bf16[128,2,2048]{0,1,2:T(2,128)(2,1)S(1)}, u32[]{:S(2)}, u32[]{:S(2)}) %all-to-all-start) | async-done | bytes 1048608 | tf_op jit(solution)/shard_map/all_to_all | solution.py:103
  68.6 1.1 copy.74
  69.7 1.5 copy.75
  71.2 1.0 fusion.40
  72.2 1.3 copy.81
  73.5 0.3 copy.84
  73.8 2.0 copy.76
  75.8 1.8 convert_reduce_fusion
  77.6 2.0 fusion.4
  79.6 3.6 fusion.35
  83.2 1.4 reshape.153
  84.6 4.0 fusion.37
  88.6 2.3 reshape.151
  90.8 3.9 convolution_convert_fusion
  94.7 1.9 copy.85
  96.6 2.3 fusion.41
  98.9 0.4 subtract_convert_fusion.1
  99.4 0.9 fusion.16
  100.3 0.0 copy-done.8
  100.4 2.7 fusion.43
  103.1 1.1 fusion.10
  104.2 2.7 fusion.44
  106.9 0.0 reduce-scatter.3.cloned.1.call-update
  106.9 0.3 all-gather.8.cloned.1.call-start
  107.2 62.8 %reduce-scatter.3.cloned.1.call-done = f32[96,2048]{1,0:T(8,128)} async-done(((f32[384,2048]{1,0:T(8,128)}), f32[96,2048]{1,0:T(8,128)}) %reduce-scatter.3.cloned.1.call-update) | async-done | bytes 786448 | tf_op jit(solution)/shard_map/reduce_scatter | solution.py:126
  169.9 1.3 convert_reduce_fusion.1
  171.3 0.3 fusion.22
  171.5 1.0 fusion.23
  172.5 0.0 all-gather.8.cloned.1.call-update
  172.6 0.0 all-gather.10.cloned.1.call-start
  172.6 0.5 all-gather.10.cloned.1.call-update
  173.1 0.0 all-gather.12.cloned.1.call-start
  173.2 0.5 all-gather.12.cloned.1.call-update
  173.7 0.0 all-gather.14.cloned.1.call-start
  173.8 0.5 all-gather.14.cloned.1.call-update
  174.3 0.0 reduce-scatter.5.cloned.1.call-start
  174.3 27.1 %all-gather.8.cloned.1.call-done = bf16[384,2048]{1,0:T(8,128)(2,1)} async-done(((bf16[96,2048]{1,0:T(8,128)(2,1)}), bf16[384,2048]{1,0:T(8,128)(2,1)}) %all-gather.8.cloned.1.call-update) | async-done | bytes 1572880 | tf_op jit(solution)/shard_map/all_gather | solution.py:134
  201.5 71.4 %all-gather.10.cloned.1.call-done = bf16[2048,2048]{1,0:T(8,128)(2,1)} async-done(((bf16[64,2048]{1,0:T(8,128)(2,1)}), bf16[2048,2048]{1,0:T(8,128)(2,1)}) %all-gather.10.cloned.1.call-update) | async-done | bytes 8388624 | tf_op jit(solution)/shard_map/all_gather | solution.py:139
  272.9 9.0 %fusion.45 = f32[384,2048]{1,0:T(8,128)} fusion(bf16[384,2048]{1,0:T(8,128)(2,1)} %all-gather.8.cloned.1.call-done, bf16[2048,2048]{1,0:T(8,128)(2,1)} %all-gather.10.cloned.1.call-done), kind=kOutput, calls=%fused_computation.76 | convolution fusion | flops 3221225472 | bytes 13107200 | tf_op jit(solution)/shard_map/dot_general | solution.py:137
  281.9 60.6 %all-gather.12.cloned.1.call-done = bf16[2048,2048]{1,0:T(8,128)(2,1)} async-done(((bf16[64,2048]{1,0:T(8,128)(2,1)}), bf16[2048,2048]{1,0:T(8,128)(2,1)}) %all-gather.12.cloned.1.call-update) | async-done | bytes 8388624 | tf_op jit(solution)/shard_map/all_gather | solution.py:140
  342.5 69.7 %all-gather.14.cloned.1.call-done = bf16[2048,2048]{1,0:T(8,128)(2,1)} async-done(((bf16[64,2048]{1,0:T(8,128)(2,1)}), bf16[2048,2048]{1,0:T(8,128)(2,1)}) %all-gather.14.cloned.1.call-update) | async-done | bytes 8388624 | tf_op jit(solution)/shard_map/all_gather | solution.py:144
  412.2 15.9 %fusion.25 = f32[384,2048]{1,0:T(8,128)} fusion(bf16[2048,2048]{1,0:T(8,128)(2,1)} %all-gather.14.cloned.1.call-done, f32[384,2048]{1,0:T(8,128)} %fusion.45, bf16[384,2048]{1,0:T(8,128)(2,1)} %all-gather.8.cloned.1.call-done, bf16[2048,2048]{1,0:T(8,128)(2,1)} %all-gather.12.cloned.1.call-done), kind=kOutput, calls=%fused_computation.42 | convolution fusion | flops 6447169536 | bytes 24641536 | tf_op jit(solution)/shard_map/dot_general | solution.py:142
  428.1 0.0 reduce-scatter.5.cloned.1.call-update
  428.1 39.4 %reduce-scatter.5.cloned.1.call-done = f32[96,2048]{1,0:T(8,128)} async-done(((f32[384,2048]{1,0:T(8,128)}), f32[96,2048]{1,0:T(8,128)}) %reduce-scatter.5.cloned.1.call-update) | async-done | bytes 786448 | tf_op jit(solution)/shard_map/reduce_scatter | solution.py:148
  467.5 2.0 fusion.24
  (27 shorter events, 0.1 us)
Async XLA Ops:
  6.5 97.6 %copy-start = (bf16[512,2048]{1,0:T(8,128)(2,1)S(1)}, bf16[512,2048]{1,0:T(8,128)(2,1)}, u32[]{:S(2)}) copy-start(bf16[512,2048]{1,0:T(8,128)(2,1)} %param.20) | copy-start | bytes 6291460
  6.5 69.3 %all-gather.6.cloned.1.call-start = ((), (), s32[]{:S(2)}) async-start(), calls=%async_computation.3 | async-start | bytes 1966080 | tf_op jit(solution)/shard_map/all_gather | solution.py:108
  8.3 36.3 %collective-permute-start = (bf16[128,4096]{0,1:T(8,128)(2,1)S(1)}, bf16[128,4096]{0,1:T(8,128)(2,1)}, u32[]{:S(2)}, u32[]{:S(2)}) collective-permute-start(bf16[128,4096]{0,1:T(8,128)(2,1)S(1)} %copy.71), channel_id=1, source_target_pairs={{0,128},{128,0},{1,129},{129,1},{2,130},{130,2},{3,131},{131,3},{4... | collective-permute-start | bytes 3145736 | tf_op jit(solution)/shard_map/ppermute | solution.py:22
  54.1 14.5 %all-to-all-start = ((bf16[128,2,2048]{0,1,2:T(2,128)(2,1)}), bf16[128,2,2048]{0,1,2:T(2,128)(2,1)S(1)}, u32[]{:S(2)}, u32[]{:S(2)}) async-start(bf16[128,2,2048]{0,1,2:T(2,128)(2,1)} %copy.73), calls=%async_computation | async-start | bytes 2097152 | tf_op jit(solution)/shard_map/all_to_all | solution.py:103
  58.9 111.1 %reduce-scatter.3.cloned.1.call-start = ((), (), s32[]{:S(2)}) async-start(), calls=%async_computation.4 | async-start | bytes 3932160 | tf_op jit(solution)/shard_map/reduce_scatter | solution.py:126
  75.8 3.8 copy-start.2
  96.6 2.3 copy-start.4
  96.6 2.3 copy-start.5
  99.4 1.0 copy-start.8
  100.3 2.7 copy-start.6
  100.3 2.7 copy-start.7
  104.2 65.8 %copy-start.3 = (bf16[96,2048]{1,0:T(8,128)(2,1)S(1)}, bf16[96,2048]{1,0:T(8,128)(2,1)}, u32[]{:S(2)}) copy-start(bf16[96,2048]{1,0:T(8,128)(2,1)} %param.12) | copy-start | bytes 1179652
  106.9 94.6 %all-gather.8.cloned.1.call-start = ((), (), s32[]{:S(2)}) async-start(), calls=%async_computation.5 | async-start | bytes 1966080 | tf_op jit(solution)/shard_map/all_gather | solution.py:134
  172.6 100.3 %all-gather.10.cloned.1.call-start = ((), (), s32[]{:S(2)}) async-start(), calls=%async_computation.6 | async-start | bytes 8650752 | tf_op jit(solution)/shard_map/all_gather | solution.py:139
  173.1 169.4 %all-gather.12.cloned.1.call-start = ((), (), s32[]{:S(2)}) async-start(), calls=%async_computation.7 | async-start | bytes 8650752 | tf_op jit(solution)/shard_map/all_gather | solution.py:140
  173.7 238.5 %all-gather.14.cloned.1.call-start = ((), (), s32[]{:S(2)}) async-start(), calls=%async_computation.8 | async-start | bytes 8650752 | tf_op jit(solution)/shard_map/all_gather | solution.py:144
  174.3 293.2 %reduce-scatter.5.cloned.1.call-start = ((), (), s32[]{:S(2)}) async-start(), calls=%async_computation.9 | async-start | bytes 3932160 | tf_op jit(solution)/shard_map/reduce_scatter | solution.py:148
  412.2 57.2 %copy-start.1 = (bf16[512,2048]{1,0:T(8,128)(2,1)S(1)}, bf16[512,2048]{1,0:T(8,128)(2,1)}, u32[]{:S(2)}) copy-start(bf16[512,2048]{1,0:T(8,128)(2,1)} %param.20) | copy-start | bytes 6291460
Sparse Core Ops, SparseCore 0:
  16.3 27.0 all-gather.5
  107.0 62.8 reduce-scatter.2
  172.7 28.7 all-gather.7
  203.2 69.6 all-gather.9
  274.6 67.9 all-gather.11
  344.2 67.9 all-gather.13
  428.2 39.2 reduce-scatter.4
where the time goes:
time: 477 us; the launch traced here: 476 us
  waiting for transfers between devices  365 us (77%)
  matrix products  41 us (9%)
  local copies, waits for them, and re-layouts  27.2 us (6%)
  other arithmetic  15.6 us (3%)
  between operations  14.3 us (3%)
  starting transfers between devices  13 us (3%)
    all_gather x1, waiting for transfers between devices, local(): gate = add_rows(lax.all_gather(gate_weight, 'dp', axis=0, tiled=True))  71.4 us
    all_gather x1, waiting for transfers between devices, local(): lax.all_gather(down_weight, 'dp', axis=0, tiled=True)  69.7 us
    reduce_scatter x1, waiting for transfers between devices, local(): lax.psum_scatter(jnp.dot(mixed, output_weight, preferred_element_type=jnp...  62.8 us
    all_gather x1, waiting for transfers between devices, local(): upward = add_rows(lax.all_gather(up_weight, 'dp', axis=0, tiled=True))  60.6 us
    reduce_scatter x1, waiting for transfers between devices, local(): hidden_own = lax.psum_scatter(terms, 'mp', scatter_dimension=0, tiled=True)  39.4 us
    all_gather x1, waiting for transfers between devices, local(): normed_two = lax.all_gather(normed_own, 'mp', axis=0, tiled=True)  27.1 us
    ppermute x1, waiting for transfers between devices, swapped(): return lax.ppermute(value, axis, pairs)  25.3 us
    dot_general x1, matrix products, local(): lax.dot_general(activated, lax.all_gather(down_weight, 'dp', axis=0, tile...  15.9 us
  transfers between devices with their start and end apart: 9, of which 8 were waited for; matrix products, arithmetic and copies ran while one was open for 6% of the time, Pallas kernels for 0%

commit v1 on v0

v1 whole, which is shorter than its diff:
```python
import functools
import math

import jax
import jax.numpy as jnp
import numpy as np
from jax import lax
from jax.experimental import pallas as pl
from jax.experimental.pallas import tpu as pltpu
from jax.sharding import PartitionSpec as P

D = 2048
FF = 2048
HEADS = 4
HEAD_DIM = 128
WIDTH = HEADS * HEAD_DIM
GROUP = 384
OWN = 96
CACHE = 512
REQS = 8
EPSILON = 1e-05
ROPE_BASE = 10000.0
MESH = pl.DeviceIdType.MESH

STREAMS = (
    (0, 0, 64, True),
    (1, 0, 64, False),
    (2, 0, 32, True),
    (2, 32, 64, False),
)
N_STREAM_COPIES = 8
N_SIB_COPIES = 6
TILES = 4
TILE = D // TILES


def normalize(rows):
    center = rows - jnp.mean(rows, axis=-1, keepdims=True)
    spread = jnp.mean(center * center, axis=-1, keepdims=True)
    return center * lax.rsqrt(spread + EPSILON)


def dot(a, b, dims=(((1,), (0,)), ((), ()))):
    return lax.dot_general(a, b, dims, preferred_element_type=jnp.float32)


class Copies:
    def __init__(self, send, recv):
        self.send, self.recv, self.used, self.all = send, recv, 0, []

    def start(self, src, dst, device):
        copy = pltpu.make_async_remote_copy(
            src_ref=src,
            dst_ref=dst,
            send_sem=self.send.at[self.used],
            recv_sem=self.recv.at[self.used],
            device_id=device,
            device_id_type=MESH,
        )
        self.used += 1
        self.all.append(copy)
        copy.start()
        return copy


class Stream:
    def __init__(self, spec, net, w_ref, place, neighbours):
        self.weight, self.first, self.end, self.x_first = spec
        self.mid = (self.first + self.end) // 2
        self.net, self.w = net, w_ref
        self.zl, self.x, self.core = place
        xp, xm, zp, zm, self.sibling = neighbours
        self.near = (xp, xm) if self.x_first else (zp, zm)
        self.far = (zp, zm) if self.x_first else (xp, xm)
        self.step = 0
        self.to_sibling = []

    def at(self, near, far, lo, hi):
        x_off, z_off = (near, far) if self.x_first else (far, near)
        x = slice(None) if x_off is None else lax.rem(self.x + x_off + 4, 4)
        zl = slice(None) if z_off is None else lax.rem(self.zl + z_off + 4, 4)
        return self.w.at[self.weight, zl, x, self.core, lo:hi]

    def push(self, part, device):
        return self.net.start(part, part, device)

    def advance(self):
        lo, mid, hi = self.first, self.mid, self.end
        plus, minus = self.near
        up, down = self.far
        if self.step == 0:
            own = self.at(0, 0, lo, hi)
            self.a = (self.push(own, plus), self.push(own, minus))
        elif self.step == 1:
            self.a[0].wait_recv()
            self.a[1].wait_recv()
            self.b = (
                self.push(self.at(-1, 0, lo, mid), plus),
                self.push(self.at(1, 0, mid, hi), minus),
            )
            self.sib(self.at(-1, 0, lo, hi))
            self.sib(self.at(1, 0, lo, hi))
        elif self.step == 2:
            self.b[0].wait_recv()
            self.b[1].wait_recv()
            line = self.at(None, 0, lo, hi)
            self.c = (self.push(line, up), self.push(line, down))
            self.sib(self.at(2, 0, lo, hi))
        elif self.step == 3:
            self.c[0].wait_recv()
            self.c[1].wait_recv()
            self.d = (
                self.push(self.at(None, -1, lo, mid), up),
                self.push(self.at(None, 1, mid, hi), down),
            )
            self.sib(self.at(None, -1, lo, hi))
            self.sib(self.at(None, 1, lo, hi))
        elif self.step == 4:
            self.d[0].wait_recv()
            self.d[1].wait_recv()
            self.sib(self.at(None, 2, lo, hi))
        elif self.step == 5:
            for copy in self.to_sibling:
                copy.wait_recv()
        self.step += 1

    def sib(self, part):
        self.to_sibling.append(self.push(part, self.sibling))


def kernel(
    traded_ref,
    lengths_ref,
    tokens_ref,
    ids_ref,
    freq_ref,
    cache_ref,
    wq_ref,
    wk_ref,
    wv_ref,
    wo_ref,
    gate_ref,
    up_ref,
    down_ref,
    out_ref,
    w,
    qkv_w,
    o_w,
    cache,
    other_tokens,
    other_ids,
    normed,
    query,
    key,
    value,
    cosine,
    sine,
    bias,
    mixed,
    terms,
    send_one,
    recv_one,
    state,
    normed_two,
    hidden,
    send_two,
    recv_two,
    done,
    other_done,
    send_sem,
    recv_sem,
    local_sem,
):
    rep, dp, mp = lax.axis_index("rep"), lax.axis_index("dp"), lax.axis_index("mp")
    zl, x, core = dp // 8, lax.rem(dp // 2, 4), lax.rem(dp, 2)
    z = rep * 4 + zl

    def at_z(where):
        where = lax.rem(where + 8, 8)
        return (where // 4, (lax.rem(where, 4) * 4 + x) * 2 + core, mp)

    def at_x(where):
        return (rep, (zl * 4 + lax.rem(where + 4, 4)) * 2 + core, mp)

    sibling = (rep, (zl * 4 + x) * 2 + (1 - core), mp)
    partner = (1 - rep, dp, mp)
    peers = [(rep, dp, lax.rem(mp + k, 4)) for k in (1, 2, 3)]
    around = (at_x(x + 1), at_x(x - 1), at_z(z + 1), at_z(z - 1), sibling)

    locals_ = []

    def fetch(src, dst):
        copy = pltpu.make_async_copy(src, dst, local_sem.at[len(locals_)])
        locals_.append(copy)
        copy.start()
        return copy

    shards = [
        fetch(ref, w.at[i, zl, x, core]) for i, ref in enumerate((gate_ref, up_ref, down_ref))
    ]

    barrier = pltpu.get_barrier_semaphore()
    friends = peers + [partner] + list(around)
    for friend in friends:
        pl.semaphore_signal(barrier, inc=1, device_id=friend, device_id_type=MESH)
    pl.semaphore_wait(barrier, len(friends))

    net = Copies(send_sem, recv_sem)
    swap_ids = net.start(ids_ref, other_ids, partner)
    swap_in = net.start(tokens_ref, other_tokens, partner)
    for copy in shards:
        copy.wait()
    streams = [Stream(spec, net, w, (zl, x, core), around) for spec in STREAMS]
    for stream in streams:
        stream.advance()
    own_shard = w.at[:, zl, x, core]
    sib_own = net.start(own_shard, own_shard, sibling)
    qkv_copies = [fetch(ref, qkv_w.at[i]) for i, ref in enumerate((wq_ref, wk_ref, wv_ref))]
    o_copy = fetch(wo_ref, o_w)
    cache_rows = pl.ds(pl.multiple_of(mp * 128, 128), 128)
    cache_copies = []
    for k in range(4):
        to = lax.rem(mp + k, 4)
        for i in range(2):
            columns = pl.ds(pl.multiple_of(i * D + to * WIDTH, WIDTH), WIDTH)
            src, dst = cache_ref.at[:, columns], cache.at[i, cache_rows]
            if k == 0:
                cache_copies.append(fetch(src, dst))
            else:
                cache_copies.append(net.start(src, dst, peers[k - 1]))

    moved = traded_ref[0] == 1
    swap_ids.wait_recv()
    swap_in.wait_recv()
    tokens = jnp.where(moved, other_tokens[...], tokens_ref[...])
    own_rows = pl.ds(pl.multiple_of(mp * OWN, OWN), OWN)
    normed[own_rows, :] = normalize(tokens.astype(jnp.float32)).astype(jnp.bfloat16)
    gathers = [net.start(normed.at[own_rows], normed.at[own_rows], peer) for peer in peers]

    group = rep * 32 + dp
    ids = jnp.where(moved, other_ids[...], ids_ref[...])
    place = lax.broadcasted_iota(jnp.int32, (1, GROUP), 1)
    positions = place
    cached_place = lax.broadcasted_iota(jnp.int32, (1, CACHE), 1)
    owner = jnp.zeros((1, CACHE), jnp.int32)
    bound = 0
    for s in range(REQS):
        length = lengths_ref[group, s]
        start = jnp.sum((ids < s).astype(jnp.int32), axis=1, keepdims=True)
        positions = positions + jnp.where(ids == s, length - start, 0)
        bound = bound + length
        owner = owner + (cached_place >= bound).astype(jnp.int32)
    ids_column = jnp.transpose(jnp.broadcast_to(ids.astype(jnp.float32), (128, GROUP)))
    places_column = jnp.transpose(jnp.broadcast_to(positions.astype(jnp.float32), (128, GROUP)))
    angle = places_column * freq_ref[...]
    cosine[...] = jnp.cos(angle)
    lane = lax.broadcasted_iota(jnp.int32, (GROUP, HEAD_DIM), 1)
    wave = jnp.sin(angle)
    sine[...] = jnp.where(lane < HEAD_DIM // 2, -wave, wave)
    column = ids_column[:, :1]
    bias[:, :CACHE] = jnp.where(column == owner.astype(jnp.float32), 0.0, -1e30)
    row_at = lax.broadcasted_iota(jnp.int32, (GROUP, GROUP), 0)
    column_at = lax.broadcasted_iota(jnp.int32, (GROUP, GROUP), 1)
    same = (column == ids.astype(jnp.float32)) & (column_at <= row_at)
    bias[:, CACHE:] = jnp.where(same, 0.0, -1e30)

    for stream in streams:
        stream.advance()
    for copy in gathers:
        copy.wait_recv()
    for copy in qkv_copies:
        copy.wait()
    for stream in streams:
        stream.advance()

    @pl.loop(0, HEADS // 2)
    def _(pair):
        columns = pl.ds(pl.multiple_of(pair * 256, 256), 256)
        rows = normed[...]
        q = dot(rows, qkv_w[0, :, columns])
        k = dot(rows, qkv_w[1, :, columns])
        v = dot(rows, qkv_w[2, :, columns])
        value[:, columns] = v.astype(jnp.bfloat16)
        for source, target in ((q, query), (k, key)):
            for half in range(2):
                head = source[:, half * HEAD_DIM : (half + 1) * HEAD_DIM]
                turned = head * cosine[...] + pltpu.roll(head, HEAD_DIM // 2, 1) * sine[...]
                place_at = pl.ds(
                    pl.multiple_of(pair * 256 + half * HEAD_DIM, HEAD_DIM), HEAD_DIM
                )
                target[:, place_at] = turned.astype(jnp.bfloat16)

    for copy in cache_copies[:2]:
        copy.wait()
    for copy in cache_copies[2:]:
        copy.wait_recv()

    scale = 1.0 / math.sqrt(HEAD_DIM)

    @pl.loop(0, HEADS)
    def _(h):
        columns = pl.ds(pl.multiple_of(h * HEAD_DIM, HEAD_DIM), HEAD_DIM)
        inner = (((1,), (1,)), ((), ()))
        for block in range(3):
            rows = slice(block * 128, block * 128 + 128)
            seen = block * 128 + 128
            q = query[rows, columns]
            old = dot(q, cache[0, :, columns], inner) * scale + bias[rows, :CACHE]
            new = dot(q, key[:seen, columns], inner) * scale + bias[rows, CACHE : CACHE + seen]
            top = jnp.maximum(
                jnp.max(old, axis=1, keepdims=True), jnp.max(new, axis=1, keepdims=True)
            )
            old, new = jnp.exp(old - top), jnp.exp(new - top)
            total = jnp.sum(old, axis=1, keepdims=True) + jnp.sum(new, axis=1, keepdims=True)
            share = 1.0 / total
            out = dot((old * share).astype(jnp.bfloat16), cache[1, :, columns])
            out = out + dot((new * share).astype(jnp.bfloat16), value[:seen, columns])
            mixed[rows, columns] = out.astype(jnp.bfloat16)

    o_copy.wait()

    def scatter(tile, part, send, recv):
        columns = slice(tile * TILE, (tile + 1) * TILE)
        terms[:, columns] = part
        send[:, columns] = part.astype(jnp.bfloat16)
        copies = []
        for k in (1, 2, 3):
            rows = pl.ds(pl.multiple_of(lax.rem(mp + k, 4) * OWN, OWN), OWN)
            copies.append(
                net.start(send.at[rows, columns], recv.at[k - 1, :, columns], peers[k - 1])
            )
        return copies

    def collect(tile, copies, recv):
        columns = slice(tile * TILE, (tile + 1) * TILE)
        for copy in copies:
            copy.wait_recv()
        total = terms[own_rows, columns]
        for k in range(3):
            total = total + recv[k, :, columns].astype(jnp.float32)
        return total

    scattered = []
    for tile in range(TILES):
        part = dot(mixed[...], o_w[:, tile * TILE : (tile + 1) * TILE])
        scattered.append(scatter(tile, part, send_one, recv_one))

    for stream in streams:
        stream.advance()

    for tile in range(TILES):
        columns = slice(tile * TILE, (tile + 1) * TILE)
        own = jnp.where(moved, other_tokens[:, columns], tokens_ref[:, columns])
        total = collect(tile, scattered[tile], recv_one)
        state[:, columns] = (own.astype(jnp.float32) + total).astype(jnp.bfloat16)
    normed_two[own_rows, :] = normalize(state[...].astype(jnp.float32)).astype(jnp.bfloat16)
    gathers = [
        net.start(normed_two.at[own_rows], normed_two.at[own_rows], peer) for peer in peers
    ]

    for stream in streams:
        stream.advance()
    for stream in streams:
        stream.advance()
    sib_own.wait_recv()
    for copy in gathers:
        copy.wait_recv()

    @pl.loop(0, FF // 256)
    def _(tile):
        columns = pl.ds(pl.multiple_of(tile * 256, 256), 256)
        rows = normed_two[...]
        gate = dot(rows, w[0, :, :, :, :, columns].reshape(D, 256))
        upward = dot(rows, w[1, :, :, :, :, columns].reshape(D, 256))
        hidden[:, columns] = (gate / (1.0 + jnp.exp(-gate)) * upward).astype(jnp.bfloat16)

    scattered = []
    for tile in range(TILES):
        part = dot(
            hidden[...], w[2, tile].reshape(TILE, FF), (((1,), (1,)), ((), ()))
        )
        scattered.append(scatter(tile, part, send_two, recv_two))
    returns = []
    for tile in range(TILES):
        columns = slice(tile * TILE, (tile + 1) * TILE)
        total = collect(tile, scattered[tile], recv_two)
        done[:, columns] = (state[:, columns].astype(jnp.float32) + total).astype(jnp.bfloat16)
        returns.append(
            net.start(done.at[:, columns], other_done.at[:, columns], partner)
        )
    for tile in range(TILES):
        columns = slice(tile * TILE, (tile + 1) * TILE)
        returns[tile].wait_recv()
        out_ref[:, columns] = jnp.where(moved, other_done[:, columns], done[:, columns])
    for copy in net.all:
        copy.wait_send()


N_COPIES = 2 + (N_STREAM_COPIES + N_SIB_COPIES) * len(STREAMS) + 1 + 6 + 3 + 3 * TILES + 3 + 3 * TILES + TILES


def local(
    tokens,
    request_ids,
    cache_entries,
    cached_lengths,
    traded,
    query_weight,
    key_weight,
    value_weight,
    output_weight,
    gate_weight,
    up_weight,
    down_weight,
):
    half = HEAD_DIM // 2
    freq = ROPE_BASE ** (-np.arange(half, dtype=np.float64) / half)
    freq = jnp.asarray(np.concatenate([freq, freq])[None].astype(np.float32))
    bf16, f32 = jnp.bfloat16, jnp.float32
    in_vmem = pl.BlockSpec(memory_space=pltpu.VMEM)
    in_smem = pl.BlockSpec(memory_space=pltpu.SMEM)
    in_hbm = pl.BlockSpec(memory_space=pl.ANY)
    return pl.pallas_call(
        kernel,
        out_shape=jax.ShapeDtypeStruct((OWN, D), bf16),
        in_specs=[in_smem, in_smem, in_vmem, in_vmem, in_vmem] + [in_hbm] * 8,
        out_specs=in_vmem,
        scratch_shapes=[
            pltpu.VMEM((3, 4, 4, 2, 64, D), bf16),
            pltpu.VMEM((3, D, WIDTH), bf16),
            pltpu.VMEM((WIDTH, D), bf16),
            pltpu.VMEM((2, CACHE, WIDTH), bf16),
            pltpu.VMEM((OWN, D), bf16),
            pltpu.VMEM((1, GROUP), jnp.int32),
            pltpu.VMEM((GROUP, D), bf16),
            pltpu.VMEM((GROUP, WIDTH), bf16),
            pltpu.VMEM((GROUP, WIDTH), bf16),
            pltpu.VMEM((GROUP, WIDTH), bf16),
            pltpu.VMEM((GROUP, HEAD_DIM), f32),
            pltpu.VMEM((GROUP, HEAD_DIM), f32),
            pltpu.VMEM((GROUP, CACHE + GROUP), f32),
            pltpu.VMEM((GROUP, WIDTH), bf16),
            pltpu.VMEM((GROUP, D), f32),
            pltpu.VMEM((GROUP, D), bf16),
            pltpu.VMEM((3, OWN, D), bf16),
            pltpu.VMEM((OWN, D), bf16),
            pltpu.VMEM((GROUP, D), bf16),
            pltpu.VMEM((GROUP, FF), bf16),
            pltpu.VMEM((GROUP, D), bf16),
            pltpu.VMEM((3, OWN, D), bf16),
            pltpu.VMEM((OWN, D), bf16),
            pltpu.VMEM((OWN, D), bf16),
            pltpu.SemaphoreType.DMA((N_COPIES,)),
            pltpu.SemaphoreType.DMA((N_COPIES,)),
            pltpu.SemaphoreType.DMA((9,)),
        ],
        compiler_params=pltpu.CompilerParams(
            collective_id=0, has_side_effects=True, vmem_limit_bytes=60 * 1024 * 1024
        ),
        name="layer",
    )(
        traded,
        cached_lengths,
        tokens,
        request_ids,
        freq,
        cache_entries,
        query_weight,
        key_weight,
        value_weight,
        output_weight,
        gate_weight,
        up_weight,
        down_weight,
    )


def solution(mesh):
    in_specs = (
        P(("rep", "dp", "mp"), None),
        P(("rep", "dp"), None),
        P(("rep", "dp", "mp"), None),
        P(),
        P("dp"),
        P(None, "mp"),
        P(None, "mp"),
        P(None, "mp"),
        P("mp", None),
        P("dp", "mp"),
        P("dp", "mp"),
        P("dp", "mp"),
    )
    out_specs = P(("rep", "dp", "mp"), None)
    return jax.shard_map(local, mesh=mesh, in_specs=in_specs, out_specs=out_specs, check_vma=False)
```

time: 477 us -> 145 us (0.30)
  waiting for transfers between devices: 365 us -> 0 us
  Pallas kernels: 0 us -> 141 us
  matrix products: 41 us -> 0 us
  local copies, waits for them, and re-layouts: 27.2 us -> 3.15 us
  other arithmetic: 15.6 us -> 0 us
  between operations: 14.3 us -> 0.66 us
  starting transfers between devices: 13 us -> 0 us
    all_gather x5 -> x0, waiting for transfers between devices: 229 us -> none  [the longest x1 71.4 us: local(): gate = add_rows(lax.all_gather(gate_weight, 'dp', axis=0, tiled=True))]
    pallas_call x0 -> x1, Pallas kernels: none -> 141 us  [local(): pl.pallas_call(kernel, out_shape=jax.ShapeDtypeStruct((OWN, D), bf16), in...]
    reduce_scatter x2 -> x0, waiting for transfers between devices: 102 us -> none  [the longest x1 62.8 us: local(): lax.psum_scatter(jnp.dot(mixed, output_weight, preferred_element_type=jnp...]
    dot_general x8 -> x0, matrix products: 41 us -> none  [the longest x1 15.9 us: local(): lax.dot_general(activated, lax.all_gather(down_weight, 'dp', axis=0, tile...]
    ppermute x1 -> x0, waiting for transfers between devices: 25.3 us -> none  [swapped(): return lax.ppermute(value, axis, pairs)]
    reshape x4 -> x0, local copies, waits for them, and re-layouts: 15 us -> none  [the longest x1 9.46 us: local(): stored.reshape(stored.shape[0], 2, D)]
    ppermute x1 -> x0, starting transfers between devices: 7.83 us -> none  [swapped(): return lax.ppermute(value, axis, pairs)]
    all_to_all x1 -> x0, waiting for transfers between devices: 7.32 us -> none  [local(): lax.all_to_all(stored.reshape(stored.shape[0], 2, D), 'mp', split_axis=2,...]
  transfers between devices with their start and end apart: 9 -> 0, of which waited for: 8 -> 0; matrix products, arithmetic and copies ran while one was open for 6% -> 0% of each run, Pallas kernels for 0% -> 0%
where the time goes in v1:
time: 145 us
  Pallas kernels  141 us (97%)
  local copies, waits for them, and re-layouts  3.15 us (2%)
    pallas_call x1, Pallas kernels, local(): pl.pallas_call(kernel, out_shape=jax.ShapeDtypeStruct((OWN, D), bf16), in...  141 us
    unnamed x2, local copies, waits for them, and re-layouts  3.15 us

profile of v1, /device:TPU:1, one launch (start us, length us, event | category | flops | bytes accessed | tf_op | source)
XLA Modules:
  0.0 145.0 jit_solution(4288514802197280989)
XLA Ops:
  0.7 1.4 copy.14.lengths_ref
  2.0 141.2 %layer.1 = bf16[96,2048]{1,0:T(8,128)(2,1)} custom-call(s32[1]{0:T(128)S(6)} %copy.16.traded_ref, s32[64,8]{1,0:T(8,128)} %copy.14.lengths_ref, bf16[96,2048]{1,0:T(8,128)(2,1)} %tokens_ref.1, s32[1,384]{1,0:T(1,128)} %ids_ref.1, f32[1,128]{1,0:T(1,128)} %constant.2.clone.freq_ref, bf16[128,4096]{1,0:T(8,128)(2,1)} %cache_ref.1, bf16[2048,512]{1,0:T(8,128)(2,1)} %wq_ref.1, ...), custom_call_target="tpu_custom_call" | custom-call | tf_op jit(solution)/shard_map/layer/pallas_call | solution.py:423
  143.3 1.8 %copy.17 = bf16[96,2048]{1,0:T(8,128)(2,1)} copy(bf16[96,2048]{1,0:T(8,128)(2,1)} %layer.1) | data formatting | bytes 786432

commit v2 on v1

v2 whole, which is shorter than its diff:
```python
import functools
import math

import jax
import jax.numpy as jnp
import numpy as np
from jax import lax
from jax.experimental import pallas as pl
from jax.experimental.pallas import tpu as pltpu
from jax.sharding import PartitionSpec as P

D = 2048
FF = 2048
HEADS = 4
HEAD_DIM = 128
WIDTH = HEADS * HEAD_DIM
GROUP = 384
OWN = 96
CACHE = 512
REQS = 8
EPSILON = 1e-05
ROPE_BASE = 10000.0
MESH = pl.DeviceIdType.MESH

STREAMS = ((0, 0, 64, True), (1, 0, 64, False), (2, 0, 64, False))
SIBLING = {"s0": (0, 3), "s1": (3, 5), "s2": (5, 6)}
PLAN = {
    "issue": ("g.start_near", "u.start_far", "g.start_far", "d.start_far",),
    "swap0": (),
    "swap1": ("u.start_near",),
    "swap2": ("g.e1",),
    "ag1": ("g.e2", "u.e3",),
    "qkv": ("u.e1", "g.e3",),
    "attn0": (),
    "attn1": ("u.e2",),
    "rs0": ("u.e4", "d.start_near",),
    "rs1": ("g.e4", "u.e5", "d.e1",),
    "ag2": ("g.e5", "d.e3", "d.e2", "g.e6", "u.e6", "g.e7", "u.e7",),
    "up0": ("d.e4",),
    "up1": ("d.e5",),
    "tile0": ("d.s0",),
    "tile1": ("d.s1", "d.e6",),
    "tile3": ("d.s2",),
}
N_STREAM_COPIES = 26
HALF = GROUP // 2
PART = OWN // 2
CHUNKS = 3
CHUNK = OWN // CHUNKS
LAG = 2
TILE = 512


def normalize(rows):
    center = rows - jnp.mean(rows, axis=-1, keepdims=True)
    spread = jnp.mean(center * center, axis=-1, keepdims=True)
    return center * lax.rsqrt(spread + EPSILON)


def dot(a, b, dims=(((1,), (0,)), ((), ()))):
    return lax.dot_general(a, b, dims, preferred_element_type=jnp.float32)


class Copies:
    def __init__(self, send, recv):
        self.send, self.recv, self.used, self.all, self.gone = send, recv, 0, [], []

    def start(self, src, dst, device):
        copy = pltpu.make_async_remote_copy(
            src_ref=src,
            dst_ref=dst,
            send_sem=self.send.at[self.used],
            recv_sem=self.recv.at[self.used],
            device_id=device,
            device_id_type=MESH,
        )
        self.used += 1
        self.all.append(copy)
        copy.start()
        return copy

    def leave(self, copies):
        for copy in copies:
            copy.wait_send()
            self.gone.append(copy)


class Stream:
    def __init__(self, spec, net, w_ref, place, neighbours):
        self.weight, self.first, self.end, self.x_first = spec
        self.mid = (self.first + self.end) // 2
        self.net, self.w = net, w_ref
        self.zl, self.x, self.core = place
        xp, xm, zp, zm, self.sibling = neighbours
        self.near = (xp, xm) if self.x_first else (zp, zm)
        self.far = (zp, zm) if self.x_first else (xp, xm)
        self.c, self.d, self.to_sibling = [None], [], []

    def at(self, near, far, lo, hi):
        x_off, z_off = (near, far) if self.x_first else (far, near)
        x = slice(None) if x_off is None else lax.rem(self.x + x_off + 4, 4)
        zl = slice(None) if z_off is None else lax.rem(self.zl + z_off + 4, 4)
        return self.w.at[self.weight, zl, x, self.core, lo:hi]

    def push(self, part, device):
        return self.net.start(part, part, device)

    def near_send(self, near, far, lo, mid, hi, halves=False):
        if halves:
            return (
                self.push(self.at(-near, far, lo, mid), self.near[0]),
                self.push(self.at(near, far, mid, hi), self.near[1]),
            )
        part = self.at(near, far, lo, hi)
        return (self.push(part, self.near[0]), self.push(part, self.near[1]))

    def far_send(self, near):
        part = self.at(near, 0, self.first, self.end)
        return (self.push(part, self.far[0]), self.push(part, self.far[1]))

    def far_pass(self, near):
        return (
            self.push(self.at(near, -1, self.first, self.mid), self.far[0]),
            self.push(self.at(near, 1, self.mid, self.end), self.far[1]),
        )

    def start_near(self):
        self.a = self.near_send(0, 0, self.first, self.mid, self.end)

    def start_far(self):
        self.c[0] = self.far_send(0)

    def e1(self):
        lo, mid, hi = self.first, self.mid, self.end
        self.wait(self.a)
        self.b = self.near_send(1, 0, lo, mid, hi, halves=True)
        self.c += [self.far_send(-1), self.far_send(1)]
        self.sib(self.at(-1, 0, lo, hi))
        self.sib(self.at(1, 0, lo, hi))

    def e2(self):
        self.wait(self.b)
        self.c.append(self.far_send(2))
        self.sib(self.at(2, 0, self.first, self.end))

    def e3(self):
        self.wait(self.c[0])
        self.d.append(self.far_pass(0))

    def e4(self):
        self.wait(self.c[1])
        self.wait(self.c[2])
        self.d += [self.far_pass(-1), self.far_pass(1)]

    def e5(self):
        self.wait(self.c[3])
        self.d.append(self.far_pass(2))
        self.sib(self.at(None, -1, self.first, self.end))
        self.sib(self.at(None, 1, self.first, self.end))

    def e6(self):
        for pair in self.d:
            self.wait(pair)
        self.sib(self.at(None, 2, self.first, self.end))

    def e7(self):
        self.from_sibling(0, 6)

    def from_sibling(self, first, end):
        for copy in self.to_sibling[first:end]:
            copy.wait_recv()

    def wait(self, pair):
        for copy in pair:
            copy.wait_recv()

    def sib(self, part):
        self.to_sibling.append(self.push(part, self.sibling))


def kernel(
    traded_ref,
    lengths_ref,
    tokens_ref,
    ids_ref,
    freq_ref,
    cache_ref,
    wq_ref,
    wk_ref,
    wv_ref,
    wo_ref,
    gate_ref,
    up_ref,
    down_ref,
    out_ref,
    w,
    qkv_w,
    o_w,
    cache,
    other_tokens,
    other_ids,
    normed,
    query,
    key,
    value,
    cosine,
    sine,
    bias,
    mixed,
    terms,
    send_one,
    recv_one,
    state,
    normed_two,
    hidden,
    sums,
    send_two,
    recv_two,
    done,
    other_done,
    send_sem,
    recv_sem,
    local_sem,
):
    rep, dp, mp = lax.axis_index("rep"), lax.axis_index("dp"), lax.axis_index("mp")
    zl, x, core = dp // 8, lax.rem(dp // 2, 4), lax.rem(dp, 2)
    z = rep * 4 + zl

    def at_z(where):
        where = lax.rem(where + 8, 8)
        return (where // 4, (lax.rem(where, 4) * 4 + x) * 2 + core, mp)

    def at_x(where):
        return (rep, (zl * 4 + lax.rem(where + 4, 4)) * 2 + core, mp)

    sibling = (rep, (zl * 4 + x) * 2 + (1 - core), mp)
    partner = (1 - rep, dp, mp)
    peers = [(rep, dp, lax.rem(mp + k, 4)) for k in (1, 2, 3)]
    around = (at_x(x + 1), at_x(x - 1), at_z(z + 1), at_z(z - 1), sibling)

    locals_ = []

    def fetch(src, dst):
        copy = pltpu.make_async_copy(src, dst, local_sem.at[len(locals_)])
        locals_.append(copy)
        copy.start()
        return copy

    shards = [
        fetch(ref, w.at[i, zl, x, core]) for i, ref in enumerate((gate_ref, up_ref, down_ref))
    ]

    barrier = pltpu.get_barrier_semaphore()
    friends = peers + [partner] + list(around)
    for friend in friends:
        pl.semaphore_signal(barrier, inc=1, device_id=friend, device_id_type=MESH)
    pl.semaphore_wait(barrier, len(friends))

    net = Copies(send_sem, recv_sem)

    def serve(place):
        for step in PLAN[place]:
            name, call = step.split(".")
            if call in SIBLING:
                streams[name].from_sibling(*SIBLING[call])
            else:
                getattr(streams[name], call)()

    swap_ids = net.start(ids_ref, other_ids, partner)
    swaps = []
    for chunk in range(CHUNKS):
        rows = slice(chunk * CHUNK, (chunk + 1) * CHUNK)
        swaps.append(net.start(tokens_ref.at[rows], other_tokens.at[rows], partner))
    cache_rows = pl.ds(pl.multiple_of(mp * 128, 128), 128)
    cache_copies = []
    for k in (2, 1, 3, 0):
        to = lax.rem(mp + k, 4)
        for i in range(2):
            columns = pl.ds(pl.multiple_of(i * D + to * WIDTH, WIDTH), WIDTH)
            src, dst = cache_ref.at[:, columns], cache.at[i, cache_rows]
            if k == 0:
                cache_copies.append(fetch(src, dst))
            else:
                cache_copies.append(net.start(src, dst, peers[k - 1]))
    for copy in shards:
        copy.wait()
    streams = {
        name: Stream(spec, net, w, (zl, x, core), around) for name, spec in zip("gud", STREAMS)
    }
    serve("issue")
    own_shard = w.at[:, zl, x, core]
    sib_own = net.start(own_shard, own_shard, sibling)
    qkv_copies = [fetch(ref, qkv_w.at[i]) for i, ref in enumerate((wq_ref, wk_ref, wv_ref))]
    o_copy = fetch(wo_ref, o_w)
    swap_ids.wait_recv()

    def kept_at(half, m):
        return slice(half * HALF + m * PART, half * HALF + (m + 1) * PART)

    def token_at(half, m):
        return slice(m * OWN + half * PART, m * OWN + (half + 1) * PART)

    blocks = [(half, m) for half in range(2) for m in range(4)]
    moved = traded_ref[0] == 1
    group = rep * 32 + dp
    ids = jnp.where(moved, other_ids[...], ids_ref[...])
    place = lax.broadcasted_iota(jnp.int32, (1, GROUP), 1)
    positions = place
    cached_place = lax.broadcasted_iota(jnp.int32, (1, CACHE), 1)
    owner = jnp.zeros((1, CACHE), jnp.int32)
    bound = 0
    for s in range(REQS):
        length = lengths_ref[s, group]
        start = jnp.sum((ids < s).astype(jnp.int32), axis=1, keepdims=True)
        positions = positions + jnp.where(ids == s, length - start, 0)
        bound = bound + length
        owner = owner + (cached_place >= bound).astype(jnp.int32)
    ids_column = jnp.transpose(jnp.broadcast_to(ids.astype(jnp.float32), (128, GROUP)))
    places_column = jnp.transpose(jnp.broadcast_to(positions.astype(jnp.float32), (128, GROUP)))
    angle = places_column * freq_ref[...]
    cosine[...] = jnp.cos(angle)
    lane = lax.broadcasted_iota(jnp.int32, (GROUP, HEAD_DIM), 1)
    wave = jnp.sin(angle)
    sine[...] = jnp.where(lane < HEAD_DIM // 2, -wave, wave)
    owner = owner.astype(jnp.float32)
    ids_row = ids.astype(jnp.float32)
    for half, m in blocks:
        column = ids_column[token_at(half, m), :1]
        kept = kept_at(half, m)
        bias[kept, :CACHE] = jnp.where(column == owner, 0.0, -1e30)
        row_at = lax.broadcasted_iota(jnp.int32, (PART, GROUP), 0) + token_at(half, m).start
        column_at = lax.broadcasted_iota(jnp.int32, (PART, GROUP), 1)
        same = (column == ids_row) & (column_at <= row_at)
        bias[kept, CACHE:] = jnp.where(same, 0.0, -1e30)

    gathers = []
    for chunk in range(CHUNKS):
        rows = slice(chunk * CHUNK, (chunk + 1) * CHUNK)
        swaps[chunk].wait_recv()
        tokens = jnp.where(moved, other_tokens[rows, :], tokens_ref[rows, :])
        kept = pl.ds(pl.multiple_of(mp * OWN + chunk * CHUNK, CHUNK), CHUNK)
        normed[kept, :] = normalize(tokens.astype(jnp.float32)).astype(jnp.bfloat16)
        for k in (2, 1, 3):
            gathers.append(net.start(normed.at[kept], normed.at[kept], peers[k - 1]))
        serve(f"swap{chunk}")
    for copy in gathers:
        copy.wait_recv()
    for copy in qkv_copies:
        copy.wait()
    serve("ag1")
    @pl.loop(0, HEADS // 2)
    def _(pair):
        columns = pl.ds(pl.multiple_of(pair * 256, 256), 256)
        rows = normed[...]
        q = dot(rows, qkv_w[0, :, columns])
        k = dot(rows, qkv_w[1, :, columns])
        v = dot(rows, qkv_w[2, :, columns])
        value[:, columns] = v.astype(jnp.bfloat16)
        for side in range(2):
            part = slice(side * HEAD_DIM, (side + 1) * HEAD_DIM)
            lanes = pl.ds(pl.multiple_of(pair * 256 + side * HEAD_DIM, HEAD_DIM), HEAD_DIM)
            turned = k[:, part] * cosine[...] + pltpu.roll(k[:, part], HEAD_DIM // 2, 1) * sine[...]
            key[:, lanes] = turned.astype(jnp.bfloat16)
            turned = q[:, part] * cosine[...] + pltpu.roll(q[:, part], HEAD_DIM // 2, 1) * sine[...]
            turned = turned.astype(jnp.bfloat16)
            for half, m in blocks:
                query[kept_at(half, m), lanes] = turned[token_at(half, m)]

    serve("qkv")
    for copy in cache_copies[:-2]:
        copy.wait_recv()
    for copy in cache_copies[-2:]:
        copy.wait()
    o_copy.wait()

    scale = 1.0 / math.sqrt(HEAD_DIM)
    own_part = [
        pl.ds(pl.multiple_of(half * HALF + mp * PART, PART), PART) for half in range(2)
    ]

    def attend(half):
        @pl.loop(0, HEADS)
        def _(h):
            columns = pl.ds(pl.multiple_of(h * HEAD_DIM, HEAD_DIM), HEAD_DIM)
            inner = (((1,), (1,)), ((), ()))
            for block in range(2):
                rows = slice(half * HALF + block * 96, half * HALF + block * 96 + 96)
                q = query[rows, columns]
                old = dot(q, cache[0, :, columns], inner) * scale + bias[rows, :CACHE]
                new = dot(q, key[:, columns], inner) * scale + bias[rows, CACHE:]
                top = jnp.maximum(
                    jnp.max(old, axis=1, keepdims=True), jnp.max(new, axis=1, keepdims=True)
                )
                old, new = jnp.exp(old - top), jnp.exp(new - top)
                total = jnp.sum(old, axis=1, keepdims=True) + jnp.sum(new, axis=1, keepdims=True)
                share = 1.0 / total
                out = dot((old * share).astype(jnp.bfloat16), cache[1, :, columns])
                out = out + dot((new * share).astype(jnp.bfloat16), value[:, columns])
                mixed[rows, columns] = out.astype(jnp.bfloat16)

    def scatter(half, columns, send, recv):
        copies = []
        for k in (2, 1, 3):
            rows = pl.ds(pl.multiple_of(half * HALF + lax.rem(mp + k, 4) * PART, PART), PART)
            copies.append(
                net.start(
                    send.at[rows, columns],
                    recv.at[k - 1, half * PART : (half + 1) * PART, columns],
                    peers[k - 1],
                )
            )
        return copies

    def collect(half, columns, copies, recv):
        for copy in copies:
            copy.wait_recv()
        total = terms[own_part[half], columns]
        for k in range(3):
            total = total + recv[k, half * PART : (half + 1) * PART, columns].astype(jnp.float32)
        return total

    def project(half):
        rows = slice(half * HALF, (half + 1) * HALF)
        for tile in range(4):
            columns = slice(tile * 512, (tile + 1) * 512)
            part = dot(mixed[rows, :], o_w[:, columns])
            terms[rows, columns] = part
            send_one[rows, columns] = part.astype(jnp.bfloat16)
        return scatter(half, slice(0, D), send_one, recv_one)

    scattered = []
    for half in range(2):
        attend(half)
        scattered.append(project(half))
        serve(f"attn{half}")


    gathers = []
    for half in range(2):
        rows = slice(half * PART, (half + 1) * PART)
        own = jnp.where(moved, other_tokens[rows, :], tokens_ref[rows, :])
        total = collect(half, slice(0, D), scattered[half], recv_one)
        fresh = (own.astype(jnp.float32) + total).astype(jnp.bfloat16)
        state[rows, :] = fresh
        kept = own_part[half]
        normed_two[kept, :] = normalize(fresh.astype(jnp.float32)).astype(jnp.bfloat16)
        gathers.append(
            [net.start(normed_two.at[kept], normed_two.at[kept], peers[k - 1]) for k in (2, 1, 3)]
        )
        serve(f"rs{half}")

    sib_own.wait_recv()
    serve("ag2")
    def raise_up(half):
        for copy in gathers[half]:
            copy.wait_recv()

        @pl.loop(0, FF // 512)
        def _(tile):
            columns = pl.ds(pl.multiple_of(tile * 512, 512), 512)
            rows = normed_two[half * HALF : (half + 1) * HALF, :]
            gate = dot(rows, w[0, :, :, :, :, columns].reshape(D, 512))
            upward = dot(rows, w[1, :, :, :, :, columns].reshape(D, 512))
            hidden[half * HALF : (half + 1) * HALF, columns] = (
                gate / (1.0 + jnp.exp(-gate)) * upward
            ).astype(jnp.bfloat16)

    raise_up(0)
    serve("up0")
    raise_up(1)
    serve("up1")
    units = [(tile, half) for tile in range(4) for half in range(2)]
    scattered = []
    returns = []

    def features(tile):
        at = lax.rem(x + (0, -1, 1, 2)[tile] + 4, 4)
        return [pl.ds(pl.multiple_of(zone * 512 + at * 128, 128), 128) for zone in range(4)]

    def give_back(unit):
        tile, half = units[unit]
        rows = slice(half * PART, (half + 1) * PART)
        for copy in scattered[unit]:
            copy.wait_recv()
        total = sums[tile, own_part[half]]
        for k in range(3):
            total = total + recv_two[k, tile, rows].astype(jnp.float32)
        base = jnp.concatenate([state[rows, lanes] for lanes in features(tile)], axis=1)
        done[tile, rows] = (base.astype(jnp.float32) + total).astype(jnp.bfloat16)
        part = net.start(done.at[tile, rows], other_done.at[tile, rows], partner)
        returns.append((tile, rows, part))

    serve("tile0")
    for unit, (tile, half) in enumerate(units):
        if half == 0 and tile in (1, 3):
            serve(f"tile{tile}")
        at = lax.rem(x + (0, -1, 1, 2)[tile] + 4, 4)
        rows = slice(half * HALF, (half + 1) * HALF)
        matrix = w[2, :, at].reshape(TILE, FF)
        part = dot(hidden[rows, :], matrix, (((1,), (1,)), ((), ())))
        sums[tile, rows] = part
        send_two[tile, rows] = part.astype(jnp.bfloat16)
        copies = []
        for k in (2, 1, 3):
            theirs = pl.ds(
                pl.multiple_of(half * HALF + lax.rem(mp + k, 4) * PART, PART), PART
            )
            target = recv_two.at[k - 1, tile, half * PART : (half + 1) * PART]
            copies.append(net.start(send_two.at[tile, theirs], target, peers[k - 1]))
        scattered.append(copies)
        if unit >= LAG:
            give_back(unit - LAG)
    for unit in range(len(units) - LAG, len(units)):
        give_back(unit)
    for tile, rows, part in returns:
        part.wait_recv()
        chosen = jnp.where(moved, other_done[tile, rows], done[tile, rows])
        for zone, lanes in enumerate(features(tile)):
            out_ref[rows, lanes] = chosen[:, zone * 128 : (zone + 1) * 128]
    for copy in net.all:
        if all(copy is not gone for gone in net.gone):
            copy.wait_send()


N_COPIES = 11 + 3 * CHUNKS + N_STREAM_COPIES * 3 + 12 + 32 + CHUNKS


def local(
    tokens,
    request_ids,
    cache_entries,
    cached_lengths,
    traded,
    query_weight,
    key_weight,
    value_weight,
    output_weight,
    gate_weight,
    up_weight,
    down_weight,
):
    half = HEAD_DIM // 2
    freq = ROPE_BASE ** (-np.arange(half, dtype=np.float64) / half)
    freq = jnp.asarray(np.concatenate([freq, freq])[None].astype(np.float32))
    bf16, f32 = jnp.bfloat16, jnp.float32
    in_vmem = pl.BlockSpec(memory_space=pltpu.VMEM)
    in_smem = pl.BlockSpec(memory_space=pltpu.SMEM)
    in_hbm = pl.BlockSpec(memory_space=pl.ANY)
    return pl.pallas_call(
        kernel,
        out_shape=jax.ShapeDtypeStruct((OWN, D), bf16),
        in_specs=[in_smem, in_smem, in_vmem, in_vmem, in_vmem] + [in_hbm] * 8,
        out_specs=in_vmem,
        scratch_shapes=[
            pltpu.VMEM((3, 4, 4, 2, 64, D), bf16),
            pltpu.VMEM((3, D, WIDTH), bf16),
            pltpu.VMEM((WIDTH, D), bf16),
            pltpu.VMEM((2, CACHE, WIDTH), bf16),
            pltpu.VMEM((OWN, D), bf16),
            pltpu.VMEM((1, GROUP), jnp.int32),
            pltpu.VMEM((GROUP, D), bf16),
            pltpu.VMEM((GROUP, WIDTH), bf16),
            pltpu.VMEM((GROUP, WIDTH), bf16),
            pltpu.VMEM((GROUP, WIDTH), bf16),
            pltpu.VMEM((GROUP, HEAD_DIM), f32),
            pltpu.VMEM((GROUP, HEAD_DIM), f32),
            pltpu.VMEM((GROUP, CACHE + GROUP), f32),
            pltpu.VMEM((GROUP, WIDTH), bf16),
            pltpu.VMEM((GROUP, D), f32),
            pltpu.VMEM((GROUP, D), bf16),
            pltpu.VMEM((3, OWN, D), bf16),
            pltpu.VMEM((OWN, D), bf16),
            pltpu.VMEM((GROUP, D), bf16),
            pltpu.VMEM((GROUP, FF), bf16),
            pltpu.VMEM((4, GROUP, TILE), f32),
            pltpu.VMEM((4, GROUP, TILE), bf16),
            pltpu.VMEM((3, 4, OWN, TILE), bf16),
            pltpu.VMEM((4, OWN, TILE), bf16),
            pltpu.VMEM((4, OWN, TILE), bf16),
            pltpu.SemaphoreType.DMA((N_COPIES,)),
            pltpu.SemaphoreType.DMA((N_COPIES,)),
            pltpu.SemaphoreType.DMA((9,)),
        ],
        compiler_params=pltpu.CompilerParams(
            collective_id=0, has_side_effects=True, vmem_limit_bytes=60 * 1024 * 1024
        ),
        name="layer",
    )(
        traded,
        cached_lengths.T,
        tokens,
        request_ids,
        freq,
        cache_entries,
        query_weight,
        key_weight,
        value_weight,
        output_weight,
        gate_weight,
        up_weight,
        down_weight,
    )


def solution(mesh):
    in_specs = (
        P(("rep", "dp", "mp"), None),
        P(("rep", "dp"), None),
        P(("rep", "dp", "mp"), None),
        P(),
        P("dp"),
        P(None, "mp"),
        P(None, "mp"),
        P(None, "mp"),
        P("mp", None),
        P("dp", "mp"),
        P("dp", "mp"),
        P("dp", "mp"),
    )
    out_specs = P(("rep", "dp", "mp"), None)
    return jax.shard_map(local, mesh=mesh, in_specs=in_specs, out_specs=out_specs, check_vma=False)
```

time: 145 us -> 132 us (0.910); the launches traced: 145 us -> 130 us
  Pallas kernels: 141 us -> 128 us
    pallas_call x1, Pallas kernels: 141 us -> 128 us  [local(): pl.pallas_call(kernel, out_shape=jax.ShapeDtypeStruct((OWN, D), bf16), in...]
    unnamed x2 -> x1, local copies, waits for them, and re-layouts: 3.15 us -> 1.77 us
where the time goes in v2:
time: 132 us; the launch traced here: 130 us
  Pallas kernels  128 us (97%)
  local copies, waits for them, and re-layouts  1.77 us (1%)
    pallas_call x1, Pallas kernels, local(): pl.pallas_call(kernel, out_shape=jax.ShapeDtypeStruct((OWN, D), bf16), in...  128 us

profile of v2, /device:TPU:1, one launch (start us, length us, event | category | flops | bytes accessed | tf_op | source)
XLA Modules:
  0.0 130.4 jit_solution(6733414938843647289)
XLA Ops:
  0.7 128.0 %layer.1 = bf16[96,2048]{1,0:T(8,128)(2,1)} custom-call(s32[1]{0:T(128)S(6)} %copy.15.traded_ref, s32[8,64]{1,0:T(8,128)} %bitcast.1, bf16[96,2048]{1,0:T(8,128)(2,1)} %tokens_ref.1, s32[1,384]{1,0:T(1,128)} %ids_ref.1, f32[1,128]{1,0:T(1,128)} %constant.2.clone.freq_ref, bf16[128,4096]{1,0:T(8,128)(2,1)} %cache_ref.1, bf16[2048,512]{1,0:T(8,128)(2,1)} %wq_ref.1, ...), custom_call_target="tpu_custom_call" | custom-call | tf_op jit(solution)/shard_map/layer/pallas_call | solution.py:549
  128.7 1.8 %copy.16 = bf16[96,2048]{1,0:T(8,128)(2,1)} copy(bf16[96,2048]{1,0:T(8,128)(2,1)} %layer.1) | data formatting | bytes 786432

commit v3 on v2

--- a/solution.py
+++ b/solution.py
@@ -32,15 +32,15 @@
     "ag1": ("g.e2", "u.e3",),
     "qkv": ("u.e1", "g.e3",),
     "attn0": (),
-    "attn1": ("u.e2",),
-    "rs0": ("u.e4", "d.start_near",),
-    "rs1": ("g.e4", "u.e5", "d.e1",),
-    "ag2": ("g.e5", "d.e3", "d.e2", "g.e6", "u.e6", "g.e7", "u.e7",),
-    "up0": ("d.e4",),
-    "up1": ("d.e5",),
+    "attn1": ("u.e2", "d.start_near",),
+    "rs0": ("u.e4",),
+    "rs1": ("g.e4", "u.e5",),
+    "ag2": ("g.e5", "d.e1", "g.e6", "u.e6", "d.e3", "d.e2", "g.e7", "u.e7",),
+    "up0": (),
+    "up1": ("d.e4",),
     "tile0": ("d.s0",),
-    "tile1": ("d.s1", "d.e6",),
-    "tile3": ("d.s2",),
+    "tile1": ("d.e5", "d.s1",),
+    "tile3": ("d.e6", "d.s2",),
 }
 N_STREAM_COPIES = 26
 HALF = GROUP // 2
@@ -333,6 +333,12 @@
         same = (column == ids_row) & (column_at <= row_at)
         bias[kept, CACHE:] = jnp.where(same, 0.0, -1e30)
 
+    def hand_on(ref, rows, side):
+        return net.start(ref.at[rows], ref.at[rows], peers[(0, 2)[side]])
+
+    def neighbour(off, first, count):
+        return pl.ds(pl.multiple_of(lax.rem(mp + off + 4, 4) * OWN + first, 16), count)
+
     gathers = []
     for chunk in range(CHUNKS):
         rows = slice(chunk * CHUNK, (chunk + 1) * CHUNK)
@@ -340,10 +346,20 @@
         tokens = jnp.where(moved, other_tokens[rows, :], tokens_ref[rows, :])
         kept = pl.ds(pl.multiple_of(mp * OWN + chunk * CHUNK, CHUNK), CHUNK)
         normed[kept, :] = normalize(tokens.astype(jnp.float32)).astype(jnp.bfloat16)
-        for k in (2, 1, 3):
-            gathers.append(net.start(normed.at[kept], normed.at[kept], peers[k - 1]))
+        gathers.append([net.start(normed.at[kept], normed.at[kept], peers[k - 1]) for k in (1, 3)])
+        if chunk == CHUNKS - 1:
+            gathers[0][0].wait_recv()
+            passed = [hand_on(normed, neighbour(-1, 0, CHUNK), 0)]
         serve(f"swap{chunk}")
-    for copy in gathers:
+    gathers[1][1].wait_recv()
+    passed.append(hand_on(normed, neighbour(1, CHUNK, CHUNK), 1))
+    gathers[2][0].wait_recv()
+    passed.append(hand_on(normed, neighbour(-1, 2 * CHUNK, CHUNK // 2), 0))
+    gathers[2][1].wait_recv()
+    passed.append(hand_on(normed, neighbour(1, 2 * CHUNK + CHUNK // 2, CHUNK // 2), 1))
+    gathers[0][1].wait_recv()
+    gathers[1][0].wait_recv()
+    for copy in passed:
         copy.wait_recv()
     for copy in qkv_copies:
         copy.wait()
@@ -445,10 +461,18 @@
         kept = own_part[half]
         normed_two[kept, :] = normalize(fresh.astype(jnp.float32)).astype(jnp.bfloat16)
         gathers.append(
-            [net.start(normed_two.at[kept], normed_two.at[kept], peers[k - 1]) for k in (2, 1, 3)]
+            [net.start(normed_two.at[kept], normed_two.at[kept], peers[k - 1]) for k in (1, 3)]
         )
-        serve(f"rs{half}")
-
+        if half == 0:
+            serve("rs0")
+
+    for half, off in enumerate((-1, 1)):
+        gathers[half].pop(half).wait_recv()
+        theirs = pl.ds(
+            pl.multiple_of(half * HALF + lax.rem(mp + off + 4, 4) * PART, PART), PART
+        )
+        gathers[half].append(hand_on(normed_two, theirs, half))
+    serve("rs1")
     sib_own.wait_recv()
     serve("ag2")
     def raise_up(half):
@@ -522,7 +546,7 @@
             copy.wait_send()
 
 
-N_COPIES = 11 + 3 * CHUNKS + N_STREAM_COPIES * 3 + 12 + 32 + CHUNKS
+N_COPIES = 12 + 3 * CHUNKS + N_STREAM_COPIES * 3 + 12 + 32 + CHUNKS
 
 
 def local(

time: 132 us -> 131 us (level); the launches traced: 130 us -> 131 us
  no operation moved by 1% of the time
where the time goes in v3:
time: 131 us
  Pallas kernels  129 us (98%)
  local copies, waits for them, and re-layouts  1.77 us (1%)
    pallas_call x1, Pallas kernels, local(): pl.pallas_call(kernel, out_shape=jax.ShapeDtypeStruct((OWN, D), bf16), in...  129 us

profile of v3, /device:TPU:1, one launch (start us, length us, event | category | flops | bytes accessed | tf_op | source)
XLA Modules:
  0.0 131.0 jit_solution(8466306441540435386)
XLA Ops:
  0.7 128.5 %layer.1 = bf16[96,2048]{1,0:T(8,128)(2,1)} custom-call(s32[1]{0:T(128)S(6)} %copy.15.traded_ref, s32[8,64]{1,0:T(8,128)} %bitcast.1, bf16[96,2048]{1,0:T(8,128)(2,1)} %tokens_ref.1, s32[1,384]{1,0:T(1,128)} %ids_ref.1, f32[1,128]{1,0:T(1,128)} %constant.2.clone.freq_ref, bf16[128,4096]{1,0:T(8,128)(2,1)} %cache_ref.1, bf16[2048,512]{1,0:T(8,128)(2,1)} %wq_ref.1, ...), custom_call_target="tpu_custom_call" | custom-call | tf_op jit(solution)/shard_map/layer/pallas_call | solution.py:573
  129.2 1.8 %copy.16 = bf16[96,2048]{1,0:T(8,128)(2,1)} copy(bf16[96,2048]{1,0:T(8,128)(2,1)} %layer.1) | data formatting | bytes 786432

commit v4 on v3

--- a/solution.py
+++ b/solution.py
@@ -47,7 +47,7 @@
 PART = OWN // 2
 CHUNKS = 3
 CHUNK = OWN // CHUNKS
-LAG = 2
+LAG = 3
 TILE = 512
 
 

time: 131 us -> 131 us (level)
  Pallas kernels: 129 us -> 127 us
where the time goes in v4:
time: 131 us; the launch traced here: 130 us
  Pallas kernels  127 us (97%)
  local copies, waits for them, and re-layouts  1.77 us (1%)
    pallas_call x1, Pallas kernels, local(): pl.pallas_call(kernel, out_shape=jax.ShapeDtypeStruct((OWN, D), bf16), in...  127 us

profile of v4, /device:TPU:1, one launch (start us, length us, event | category | flops | bytes accessed | tf_op | source)
XLA Modules:
  0.0 129.9 jit_solution(16083523161165300417)
XLA Ops:
  0.7 127.5 %layer.1 = bf16[96,2048]{1,0:T(8,128)(2,1)} custom-call(s32[1]{0:T(128)S(6)} %copy.15.traded_ref, s32[8,64]{1,0:T(8,128)} %bitcast.1, bf16[96,2048]{1,0:T(8,128)(2,1)} %tokens_ref.1, s32[1,384]{1,0:T(1,128)} %ids_ref.1, f32[1,128]{1,0:T(1,128)} %constant.2.clone.freq_ref, bf16[128,4096]{1,0:T(8,128)(2,1)} %cache_ref.1, bf16[2048,512]{1,0:T(8,128)(2,1)} %wq_ref.1, ...), custom_call_target="tpu_custom_call" | custom-call | tf_op jit(solution)/shard_map/layer/pallas_call | solution.py:573
  128.1 1.8 %copy.16 = bf16[96,2048]{1,0:T(8,128)(2,1)} copy(bf16[96,2048]{1,0:T(8,128)(2,1)} %layer.1) | data formatting | bytes 786432
